TPU v7x, 32 devices: a whole 2x2x4 slice. The times are simulated.
32 devices in a mesh: gz: 2 (over y), row: 4 (over x, core), col: 4 (over z).
Axes of the slice: x: 2, y: 2, z: 4, core: 2. Of those that a mesh axis runs over, the one named last changes fastest.
Arguments:
- anc_lower: bfloat16 [1, 1024, 1024], P(None, 'col', 'row'), may hold values from -0.125 to 0.125
- anc_upper: bfloat16 [1, 1024, 1024], P(None, 'col', 'row'), may hold values from -0.125 to 0.125
- sub_lower: bfloat16 [16, 1024, 1024], P('gz', 'col', 'row'), may hold values from -0.125 to 0.125
- sub_upper: bfloat16 [16, 1024, 1024], P('gz', 'col', 'row'), may hold values from -0.125 to 0.125
- anc_rhs: bfloat16 [1, 1024, 64], P(None, 'col'), may hold values from -6 to 6
- sub_rhs: bfloat16 [6, 1024, 64], P('gz', 'col'), may hold values from -6 to 6
- layer_subtree: int32 [2], replicated, may hold values from 0 to 1, each once
- sub_pattern: int32 [10, 2], P('gz'), may hold values 0 or 1
Outputs:
- anc_solution: float32 [1, 1024, 64], P(None, ('row', 'col'))
- sub_solution: float32 [6, 1024, 64], P('gz', ('row', 'col'))
Inputs may be any that keep to these rules, and one draw needn't show every extreme that they name: `layer_subtree`: each subtree is held by exactly one layer.
All inputs are finite; a program needn't handle non-finite values. No bound on the sum of `sub_pattern` on one device may be relied on, other than what follows from the above.
Results may differ from a plain program's by a relative error of at most 0.018.
Values may be sent and summed in bfloat16 or wider, within the bound.
A program may use at most 64 MiB of HBM per device.

v0:
```python
import jax
import jax.numpy as jnp
import numpy as np
from jax import lax
from jax.sharding import PartitionSpec as P

R = 64
SUB_LEVELS = 2
SUB_NODES = 3


def level_span(depth_now):
    return (2**depth_now - 1, 2 ** (depth_now + 1) - 1)


def local_routes(first_id, stop_id, depth_now, target_count):
    table = np.zeros((target_count, (stop_id - first_id) * depth_now), np.float32)
    for offset, member in enumerate(range(first_id, stop_id)):
        for local_level in range(depth_now):
            target = (member + 1 >> depth_now - local_level) - 1
            table[target, offset * depth_now + local_level] = 1.0
    return table


def solve_diagonal(residual, blocks):
    whole_blocks = lax.all_gather(blocks, "col", axis=1, tiled=True)
    whole_res = lax.all_gather(residual, "col", axis=1, tiled=True)
    rows_full = jnp.einsum(
        "nki,nkr->nir", whole_blocks, whole_res, preferred_element_type=jnp.float32
    )
    share = rows_full.shape[1] // lax.axis_size("col")
    owned = lax.dynamic_slice_in_dim(rows_full, lax.axis_index("col") * share, share, 1)
    return (owned, rows_full.astype(jnp.bfloat16))


def upper_sum(values):
    return lax.psum(values, "row")


def local(anc_lower, anc_upper, sub_lower, sub_upper, anc_rhs, sub_rhs, layer_subtree, sub_pattern):
    layers = lax.axis_size("gz")
    levels = layers.bit_length() - 1
    anc_count = layers - 1
    row_count = lax.axis_size("row")
    col_count = lax.axis_size("col")
    rows_here = anc_lower.shape[2]
    cols_here = anc_lower.shape[1]
    sub_start = [0]
    for member in range(SUB_NODES):
        sub_start.append(sub_start[-1] + levels + (member + 1).bit_length() - 1)
    anc_start = [0]
    for member in range(anc_count):
        anc_start.append(anc_start[-1] + (member + 1).bit_length() - 1)
    low_pattern = sub_pattern[:, 0].astype(jnp.float32)
    up_pattern = sub_pattern[:, 1].astype(jnp.float32)
    layer_here = lax.axis_index("gz")
    subtree = jnp.sum(
        jnp.where(jnp.arange(layers, dtype=jnp.int32) == layer_here, layer_subtree, 0)
    )
    powers = jnp.asarray(2 ** (levels - np.arange(levels)), jnp.int32)
    heap_ids = (subtree + layers) // powers - 1
    choose = (heap_ids[:, None] == jnp.arange(anc_count, dtype=jnp.int32)[None, :]).astype(
        jnp.float32
    )
    first_layer = (layer_here == 0).astype(jnp.float32)
    row_index = lax.axis_index("row")
    col_index = lax.axis_index("col")
    holds_piece = (row_index == col_index * row_count // col_count).astype(jnp.float32)
    piece_start = jnp.clip(col_index * cols_here - row_index * rows_here, 0, rows_here - cols_here)

    def own_piece(rows_block):
        return holds_piece * lax.dynamic_slice_in_dim(rows_block, piece_start, cols_here, 1).astype(
            jnp.float32
        )

    sub_acc = jnp.zeros((SUB_NODES, cols_here, R), jnp.float32)
    to_anc = jnp.zeros((anc_count, cols_here, R), jnp.float32)
    sub_rows = {}
    for depth_now in reversed(range(SUB_LEVELS)):
        first_id, stop_id = level_span(depth_now)
        node_count = stop_id - first_id
        given = sub_rhs[first_id:stop_id].astype(jnp.float32)
        if depth_now + 1 < SUB_LEVELS:
            given = given - lax.psum(sub_acc[first_id:stop_id], "row")
        unused, solved = solve_diagonal(given.astype(jnp.bfloat16), sub_lower[first_id:stop_id])
        sub_rows[depth_now] = solved
        per_node = levels + depth_now
        opening = SUB_NODES + sub_start[first_id]
        blocks = sub_lower[opening : opening + node_count * per_node].reshape(
            node_count, per_node, cols_here, rows_here
        )
        weights = low_pattern[sub_start[first_id] : sub_start[stop_id]].reshape(
            node_count, per_node
        )
        updates = jnp.einsum("npik,nkr->npir", blocks, solved, preferred_element_type=jnp.float32)
        updates = updates * weights[:, :, None, None]
        to_anc = to_anc + jnp.einsum("ea,eir->air", choose, jnp.sum(updates[:, :levels], 0))
        if depth_now > 0:
            table = jnp.asarray(local_routes(first_id, stop_id, depth_now, SUB_NODES))
            sub_acc = sub_acc + jnp.einsum(
                "tq,qir->tir", table, updates[:, levels:].reshape(-1, cols_here, R)
            )
    anc_acc = jnp.zeros((anc_count, cols_here, R), jnp.float32)
    anc_rows = {}
    for depth_now in reversed(range(levels)):
        first_id, stop_id = level_span(depth_now)
        node_count = stop_id - first_id
        joined = to_anc[first_id:stop_id] + first_layer * anc_acc[first_id:stop_id]
        reached = lax.psum(joined, ("gz", "row"))
        given = anc_rhs[first_id:stop_id].astype(jnp.float32) - reached
        unused, solved = solve_diagonal(given.astype(jnp.bfloat16), anc_lower[first_id:stop_id])
        anc_rows[depth_now] = solved
        if depth_now > 0:
            opening = anc_count + anc_start[first_id]
            blocks = anc_lower[opening : opening + node_count * depth_now].reshape(
                node_count, depth_now, cols_here, rows_here
            )
            updates = jnp.einsum(
                "npik,nkr->npir", blocks, solved, preferred_element_type=jnp.float32
            )
            table = jnp.asarray(local_routes(first_id, stop_id, depth_now, anc_count))
            anc_acc = anc_acc + jnp.einsum("tq,qir->tir", table, updates.reshape(-1, cols_here, R))
    anc_z_parts = []
    anc_out_parts = []
    for depth_now in range(levels):
        first_id, stop_id = level_span(depth_now)
        node_count = stop_id - first_id
        given = own_piece(anc_rows[depth_now])
        if depth_now > 0:
            z_sofar = jnp.concatenate(anc_z_parts, 0)
            table = local_routes(first_id, stop_id, depth_now, anc_count)[:first_id].T
            sources = jnp.einsum(
                "qa,akr->qkr",
                jnp.asarray(table, jnp.bfloat16),
                z_sofar,
                preferred_element_type=jnp.float32,
            )
            sources = sources.astype(jnp.bfloat16).reshape(node_count, depth_now, rows_here, R)
            opening = anc_count + anc_start[first_id]
            blocks = anc_upper[opening : opening + node_count * depth_now].reshape(
                node_count, depth_now, cols_here, rows_here
            )
            updates = jnp.einsum(
                "npik,npkr->npir", blocks, sources, preferred_element_type=jnp.float32
            )
            given = given - jnp.sum(updates, 1)
        summed = upper_sum(given)
        owned, solved = solve_diagonal(summed.astype(jnp.bfloat16), anc_upper[first_id:stop_id])
        anc_out_parts.append(owned)
        anc_z_parts.append(solved)
    anc_z_all = jnp.concatenate(anc_z_parts, 0)
    selected = jnp.einsum(
        "ea,akr->ekr", choose.astype(jnp.bfloat16), anc_z_all, preferred_element_type=jnp.float32
    )
    selected = selected.astype(jnp.bfloat16)
    sub_z_parts = []
    sub_out_parts = []
    for depth_now in range(SUB_LEVELS):
        first_id, stop_id = level_span(depth_now)
        node_count = stop_id - first_id
        per_node = levels + depth_now
        opening = SUB_NODES + sub_start[first_id]
        blocks = sub_upper[opening : opening + node_count * per_node].reshape(
            node_count, per_node, cols_here, rows_here
        )
        weights = up_pattern[sub_start[first_id] : sub_start[stop_id]].reshape(node_count, per_node)
        updates = jnp.einsum(
            "npik,pkr->npir", blocks[:, :levels], selected, preferred_element_type=jnp.float32
        )
        if depth_now > 0:
            z_sofar = sub_z_parts[0]
            table = local_routes(first_id, stop_id, depth_now, SUB_NODES)[:first_id].T
            sources = jnp.einsum(
                "qa,akr->qkr",
                jnp.asarray(table, jnp.bfloat16),
                z_sofar,
                preferred_element_type=jnp.float32,
            )
            sources = sources.astype(jnp.bfloat16).reshape(node_count, depth_now, rows_here, R)
            local_updates = jnp.einsum(
                "npik,npkr->npir", blocks[:, levels:], sources, preferred_element_type=jnp.float32
            )
            updates = jnp.concatenate([updates, local_updates], 1)
        change = jnp.sum(updates * weights[:, :, None, None], 1)
        summed = upper_sum(own_piece(sub_rows[depth_now]) - change)
        owned, solved = solve_diagonal(summed.astype(jnp.bfloat16), sub_upper[first_id:stop_id])
        sub_out_parts.append(owned)
        sub_z_parts.append(solved)
    return (jnp.concatenate(anc_out_parts, 0), jnp.concatenate(sub_out_parts, 0))


def solution(mesh):
    in_specs = (
        P(None, "col", "row"),
        P(None, "col", "row"),
        P("gz", "col", "row"),
        P("gz", "col", "row"),
        P(None, "col", None),
        P("gz", "col", None),
        P(),
        P("gz", None),
    )
    out_specs = (P(None, ("row", "col"), None), P("gz", ("row", "col"), None))
    return jax.shard_map(local, mesh=mesh, in_specs=in_specs, out_specs=out_specs, check_vma=False)
```

profile of v0, /device:TPU:0, one launch (start us, length us, event | category | flops | bytes accessed | tf_op | source)
XLA Modules:
  0.0 251.9 jit_solution(8480645708661849595)
XLA Ops:
  7.2 1.7 slice.67
  11.8 17.3 %all_gather.37 = bf16[2,1024,64]{1,2,0:T(8,128)(2,1)S(1)} all-gather(bf16[2,256,64]{1,2,0:T(8,128)(2,1)S(1)} %slice-done.3), channel_id=1, replica_groups=mesh['gz'=2,'row'=4,'col'=4] {'col'}, dimensions={1}, use_global_device_ids=true | all-gather | bytes 327680 | tf_op jit(solution)/shard_map/all_gather | solution.py:27
  29.1 22.6 %all_gather.39 = bf16[1,1024,256]{2,1,0:T(8,128)(2,1)S(1)} all-gather(bf16[1,256,256]{2,1,0:T(8,128)(2,1)S(1)} %slice-done.1), channel_id=1, replica_groups=mesh['gz'=2,'row'=4,'col'=4] {'col'}, dimensions={1}, use_global_device_ids=true | all-gather | bytes 655360 | tf_op jit(solution)/shard_map/all_gather | solution.py:26
  51.7 1.6 convolution_convert_fusion
  54.0 0.9 fusion.27
  55.0 30.0 %all-reduce.4.cloned.1.call-done = f32[1,256,64]{1,0,2:T(1,128)} async-done(((f32[1,256,64]{1,0,2:T(1,128)}), f32[1,256,64]{1,0,2:T(1,128)}) %all-reduce.4.cloned.1.call-update) | async-done | bytes 65552 | tf_op jit(solution)/shard_map/psum | solution.py:84
  85.0 0.9 fusion.30
  85.9 13.5 %all_gather.38 = bf16[1,1024,64]{1,0,2:T(2,128)(2,1)S(1)} all-gather(bf16[1,256,64]{1,0,2:T(2,128)(2,1)S(1)} %fusion.30), channel_id=1, replica_groups=mesh['gz'=2,'row'=4,'col'=4] {'col'}, dimensions={1}, use_global_device_ids=true | all-gather | bytes 163840 | tf_op jit(solution)/shard_map/all_gather | solution.py:27
  99.6 0.9 fusion.7
  101.4 0.8 copy-done.3
  102.2 14.9 %all_gather.41 = bf16[1,1024,256]{2,1,0:T(8,128)(2,1)S(1)} all-gather(bf16[1,256,256]{2,1,0:T(8,128)(2,1)S(1)} %copy-done.3), channel_id=1, replica_groups=mesh['gz'=2,'row'=4,'col'=4] {'col'}, dimensions={1}, use_global_device_ids=true | all-gather | bytes 655360 | tf_op jit(solution)/shard_map/all_gather | solution.py:26
  117.1 16.3 %all_gather.43 = bf16[1,1024,256]{2,1,0:T(8,128)(2,1)S(1)} all-gather(bf16[1,256,256]{2,1,0:T(8,128)(2,1)S(1)} %copy-done.4), channel_id=1, replica_groups=mesh['gz'=2,'row'=4,'col'=4] {'col'}, dimensions={1}, use_global_device_ids=true | all-gather | bytes 655360 | tf_op jit(solution)/shard_map/all_gather | solution.py:26
  133.4 14.8 %all_gather.45 = bf16[1,1024,256]{2,1,0:T(8,128)(2,1)S(1)} all-gather(bf16[1,256,256]{2,1,0:T(8,128)(2,1)S(1)} %slice-done.2), channel_id=1, replica_groups=mesh['gz'=2,'row'=4,'col'=4] {'col'}, dimensions={1}, use_global_device_ids=true | all-gather | bytes 655360 | tf_op jit(solution)/shard_map/all_gather | solution.py:26
  148.5 2.8 %all-reduce.6.cloned.1.call-done = f32[1,256,64]{1,2,0:T(8,128)} async-done(((f32[1,256,64]{1,2,0:T(8,128)}), f32[1,256,64]{1,2,0:T(8,128)}) %all-reduce.6.cloned.1.call-update) | async-done | bytes 65552 | tf_op jit(solution)/shard_map/psum | solution.py:109
  151.3 0.8 subtract_convert_fusion
  152.1 13.9 %all_gather.40 = bf16[1,1024,64]{1,2,0:T(8,128)(2,1)S(1)} all-gather(bf16[1,256,64]{1,2,0:T(8,128)(2,1)S(1)} %subtract_convert_fusion), channel_id=1, replica_groups=mesh['gz'=2,'row'=4,'col'=4] {'col'}, dimensions={1}, use_global_device_ids=true | all-gather | bytes 163840 | tf_op jit(solution)/shard_map/all_gather | solution.py:27
  166.2 11.5 %psum.37 = bf16[1,256,64]{1,2,0:T(8,128)(2,1)S(1)} all-reduce(f32[1,256,64]{1,2,0:T(8,128)S(1)} %fusion.10), channel_id=1, replica_groups=mesh['gz'=2,'row'=4,'col'=4] {'row'}, use_global_device_ids=true, to_apply=%region_4.5 | all-reduce | flops 16384 | bytes 98304 | tf_op jit(solution)/shard_map/psum | solution.py:37
  177.7 13.4 %all_gather.42 = bf16[1,1024,64]{1,2,0:T(8,128)(2,1)S(1)} all-gather(bf16[1,256,64]{1,2,0:T(8,128)(2,1)S(1)} %psum.37), channel_id=1, replica_groups=mesh['gz'=2,'row'=4,'col'=4] {'col'}, dimensions={1}, use_global_device_ids=true | all-gather | bytes 163840 | tf_op jit(solution)/shard_map/all_gather | solution.py:27
  191.5 10.7 %psum.38 = bf16[1,256,64]{1,2,0:T(8,128)(2,1)S(1)} all-reduce(f32[1,256,64]{1,2,0:T(8,128)S(1)} %fusion.3), channel_id=1, replica_groups=mesh['gz'=2,'row'=4,'col'=4] {'row'}, use_global_device_ids=true, to_apply=%region_5.6 | all-reduce | flops 16384 | bytes 98304 | tf_op jit(solution)/shard_map/psum | solution.py:37
  202.2 13.3 %all_gather.44 = bf16[1,1024,64]{1,2,0:T(8,128)(2,1)S(1)} all-gather(bf16[1,256,64]{1,2,0:T(8,128)(2,1)S(1)} %psum.38), channel_id=1, replica_groups=mesh['gz'=2,'row'=4,'col'=4] {'col'}, dimensions={1}, use_global_device_ids=true | all-gather | bytes 163840 | tf_op jit(solution)/shard_map/all_gather | solution.py:27
  216.3 11.9 %all-reduce.7 = bf16[2,256,64]{1,2,0:T(8,128)(2,1)S(1)} all-reduce(f32[2,256,64]{1,2,0:T(8,128)S(1)} %multiply_subtract_fusion), channel_id=1, replica_groups=mesh['gz'=2,'row'=4,'col'=4] {'row'}, use_global_device_ids=true, to_apply=%region_7.8 | all-reduce | flops 32768 | bytes 196608 | tf_op jit(solution)/shard_map/psum | solution.py:37
  228.2 14.0 %all_gather.46 = bf16[2,1024,64]{1,2,0:T(8,128)(2,1)S(1)} all-gather(bf16[2,256,64]{1,2,0:T(8,128)(2,1)S(1)} %all-reduce.7), channel_id=1, replica_groups=mesh['gz'=2,'row'=4,'col'=4] {'col'}, dimensions={1}, use_global_device_ids=true | all-gather | bytes 327680 | tf_op jit(solution)/shard_map/all_gather | solution.py:27
  242.3 1.5 fusion.36
  243.9 0.7 copy.24
  (64 shorter events, 6.6 us)
Async XLA Ops:
  7.2 44.6 %all-gather.3.cloned.1.call-start = ((), (), s32[]{:S(2)}) async-start(), calls=%async_computation | async-start | bytes 1310720 | tf_op jit(solution)/shard_map/all_gather | solution.py:26
  8.9 76.1 %all-reduce.4.cloned.1.call-start = ((), (), s32[]{:S(2)}) async-start(), calls=%async_computation.1 | async-start | bytes 131072 | tf_op jit(solution)/shard_map/psum | solution.py:84
  9.0 0.7 copy-start.7
  10.9 0.9 slice-start.3
  10.9 0.7 copy-start.6
  11.8 17.3 %slice-start.1 = ((bf16[8,256,256]{2,1,0:T(8,128)(2,1)}), bf16[1,256,256]{2,1,0:T(8,128)(2,1)S(1)}, s32[]{:S(2)}) async-start(bf16[8,256,256]{2,1,0:T(8,128)(2,1)} %param.13), calls=%async_computation.5 | async-start | bytes 262144 | tf_op jit(solution)/shard_map/slice | solution.py:85
  51.7 1.6 slice-start
  53.3 0.7 copy-start.8
  53.3 31.7 %slice-start.4 = ((bf16[3,256,64]{1,2,0:T(8,128)(2,1)}), bf16[1,256,64]{1,2,0:T(8,128)(2,1)S(1)}, s32[]{:S(2)}) async-start(bf16[3,256,64]{1,2,0:T(8,128)(2,1)} %param.16), calls=%async_computation.8 | async-start | bytes 65536 | tf_op jit(solution)/shard_map/slice | solution.py:82
  53.6 46.0 %copy-start = (bf16[8,256,256]{2,1,0:T(8,128)(2,1)S(1)}, bf16[8,256,256]{2,1,0:T(8,128)(2,1)}, u32[]{:S(2)}) copy-start(bf16[8,256,256]{2,1,0:T(8,128)(2,1)} %param.13) | copy-start | bytes 3145732
  54.0 46.5 %copy-start.1 = (bf16[8,256,256]{2,1,0:T(8,128)(2,1)S(1)}, bf16[8,256,256]{2,1,0:T(8,128)(2,1)}, u32[]{:S(2)}) copy-start(bf16[8,256,256]{2,1,0:T(8,128)(2,1)} %param.14) | copy-start | bytes 3145732
  54.9 96.3 %all-reduce.6.cloned.1.call-start = ((), (), s32[]{:S(2)}) async-start(), calls=%async_computation.2 | async-start | bytes 131072 | tf_op jit(solution)/shard_map/psum | solution.py:109
  100.5 141.8 %all-gather.5.cloned.1.call-start = ((), (), s32[]{:S(2)}) async-start(), calls=%async_computation.3 | async-start | bytes 1310720 | tf_op jit(solution)/shard_map/all_gather | solution.py:26
  101.3 0.9 copy-start.3
  102.2 14.9 %copy-start.4 = (bf16[1,256,256]{2,1,0:T(8,128)(2,1)S(1)}, bf16[1,256,256]{2,1,0:T(8,128)(2,1)}, u32[]{:S(2)}) copy-start(bf16[1,256,256]{2,1,0:T(8,128)(2,1)} %param.12) | copy-start | bytes 393220
  117.1 16.3 %slice-start.2 = ((bf16[8,256,256]{2,1,0:T(8,128)(2,1)}), bf16[1,256,256]{2,1,0:T(8,128)(2,1)S(1)}, s32[]{:S(2)}) async-start(bf16[8,256,256]{2,1,0:T(8,128)(2,1)} %param.14), calls=%async_computation.6 | async-start | bytes 262144 | tf_op jit(solution)/shard_map/slice | solution.py:186
  133.4 17.9 %copy-start.5 = (bf16[1,256,64]{1,2,0:T(8,128)(2,1)S(1)}, bf16[1,256,64]{1,2,0:T(8,128)(2,1)}, u32[]{:S(2)}) copy-start(bf16[1,256,64]{1,2,0:T(8,128)(2,1)} %param.15) | copy-start | bytes 98308
  148.2 43.1 %copy-start.2 = (bf16[8,256,256]{2,1,0:T(8,128)(2,1)S(1)}, bf16[8,256,256]{2,1,0:T(8,128)(2,1)}, u32[]{:S(2)}) copy-start(bf16[8,256,256]{2,1,0:T(8,128)(2,1)} %param.14) | copy-start | bytes 3145732
Sparse Core Ops, SparseCore 0:
  9.5 40.4 all-gather.2
  55.0 29.9 all-reduce.3
  100.6 50.5 all-reduce.5
  152.7 27.7 all-gather.4
where the time goes:
time: 253 us; the launch traced here: 252 us
  blocking collectives  188 us (74%)
  waiting for transfers between devices  32.9 us (13%)
  between operations  14.7 us (6%)
  local copies, waits for them, and re-layouts  7.11 us (3%)
  matrix products  6.59 us (3%)
    all_gather x6, blocking collectives, solve_diagonal(): whole_res = lax.all_gather(residual, 'col', axis=1, tiled=True)  85.3 us
    all_gather x4, blocking collectives, solve_diagonal(): whole_blocks = lax.all_gather(blocks, 'col', axis=1, tiled=True)  68.6 us
    psum x3, blocking collectives, upper_sum(): return lax.psum(values, 'row')  34 us
    psum x1, waiting for transfers between devices, local(): given = given - lax.psum(sub_acc[first_id:stop_id], 'row')  30 us
  transfers between devices with their start and end apart: 4, of which 2 were waited for; matrix products, arithmetic and copies ran while one was open for 2% of the time, Pallas kernels for 0%

commit v1 on v0

--- a/solution.py
+++ b/solution.py
@@ -1,7 +1,11 @@
+import functools
+
 import jax
 import jax.numpy as jnp
 import numpy as np
 from jax import lax
+from jax.experimental import pallas as pl
+from jax.experimental.pallas import tpu as pltpu
 from jax.sharding import PartitionSpec as P
 
 R = 64
@@ -189,6 +193,323 @@
     return (jnp.concatenate(anc_out_parts, 0), jnp.concatenate(sub_out_parts, 0))
 
 
+BF = jnp.bfloat16
+F32 = jnp.float32
+MESH = pl.DeviceIdType.MESH
+
+
+def times(vectors, block):
+    return jnp.dot(vectors, block, preferred_element_type=F32)
+
+
+def times_t(vectors, block):
+    return lax.dot_general(vectors, block, (((1,), (1,)), ((), ())), preferred_element_type=F32)
+
+
+def flip(rows):
+    return jnp.transpose(rows.astype(F32))
+
+
+def fused_kernel(
+    layers,
+    rows_n,
+    cols_n,
+    anc_lower,
+    anc_upper,
+    sub_lower,
+    sub_upper,
+    anc_rhs,
+    sub_rhs,
+    layer_subtree,
+    pattern,
+    anc_out,
+    sub_out,
+    al,
+    au,
+    sl,
+    su,
+    ar,
+    sr,
+    pair_send,
+    pair_recv,
+    one_send,
+    one_recv,
+    all_send,
+    all_recv,
+    diag_recv,
+    flipped,
+    piece_send,
+    piece_recv,
+    load_sem,
+    send_sem,
+    recv_sem,
+):
+    gz = lax.axis_index("gz")
+    row = lax.axis_index("row")
+    col = lax.axis_index("col")
+    loads = {}
+
+    def load(name, source, target):
+        copy = pltpu.make_async_copy(source, target, load_sem.at[len(loads)])
+        copy.start()
+        loads[name] = copy
+
+    load("sr", sub_rhs, sr)
+    load("e12", sub_lower.at[pl.ds(1, 2)], sl.at[pl.ds(1, 2)])
+    load("low", sub_lower.at[pl.ds(3, 5)], sl.at[pl.ds(3, 5)])
+    load("e0", sub_lower.at[0], sl.at[0])
+    load("ar", anc_rhs, ar)
+    load("al", anc_lower, al)
+    load("au", anc_upper, au)
+    load("su", sub_upper, su)
+
+    def row_peer(j):
+        return (gz, lax.rem(row + j, rows_n), col)
+
+    def col_peer(j):
+        return (gz, row, lax.rem(col + j, cols_n))
+
+    barrier = pltpu.get_barrier_semaphore()
+    peers = [row_peer(j) for j in range(1, rows_n)] + [col_peer(j) for j in range(1, cols_n)]
+    wide = [
+        (lax.rem(gz + g, layers), lax.rem(row + j, rows_n), col)
+        for g in range(layers)
+        for j in range(rows_n)
+        if g or j
+    ]
+    peers = peers + wide[rows_n - 1 :]
+    for peer in peers:
+        pl.semaphore_signal(barrier, inc=1, device_id=peer, device_id_type=MESH)
+
+    started = []
+
+    def send(step, source, target, peer_list):
+        made = []
+        for j, peer in enumerate(peer_list):
+            copy = pltpu.make_async_remote_copy(
+                src_ref=source(j),
+                dst_ref=target(j),
+                send_sem=send_sem.at[step, j],
+                recv_sem=recv_sem.at[step, j],
+                device_id=peer,
+                device_id_type=MESH,
+            )
+            copy.start()
+            made.append(copy)
+        started.extend(made)
+        return made
+
+    def swap(step, values, peer_list, send_buf, recv_buf, between=None):
+        for n, value in enumerate(values):
+            send_buf[n] = value.astype(BF)
+        made = send(step, lambda j: send_buf, lambda j: recv_buf.at[j], peer_list)
+        extra = between() if between is not None else None
+        sums = list(values)
+        for j, copy in enumerate(made):
+            copy.wait_recv()
+            for n in range(len(sums)):
+                sums[n] = sums[n] + recv_buf[j, n].astype(F32)
+        return sums, extra
+
+    row_list = [row_peer(j) for j in range(1, rows_n)]
+    col_list = [col_peer(j) for j in range(1, cols_n)]
+
+    anc_here = jnp.where((layers + layer_subtree[gz]) // layers - 1 == 0, 1, 0)
+    low = [pattern[p, 0] for p in range(5)]
+    up = [pattern[p, 1] for p in range(5)]
+    low = [(w * anc_here if p in (0, 1, 3) else w).astype(F32) for p, w in enumerate(low)]
+    up = [(w * anc_here if p in (0, 1, 3) else w).astype(F32) for p, w in enumerate(up)]
+    on_diag = jnp.where(row == col, 1.0, 0.0).astype(F32)
+
+    loads["sr"].wait()
+    r1 = flip(sr[1]).astype(BF)
+    r2 = flip(sr[2]).astype(BF)
+    loads["e12"].wait()
+    part1 = times(r1, sl[1])
+    part2 = times(r2, sl[2])
+    pl.semaphore_wait(barrier, len(peers))
+
+    def between_a():
+        loads["ar"].wait()
+        return flip(sr[0]), flip(ar[0])
+
+    (y1, y2), (given0, given_anc) = swap(
+        0, [part1, part2], col_list, pair_send.at[0], pair_recv.at[0], between_a
+    )
+    y1 = y1.astype(BF)
+    y2 = y2.astype(BF)
+    loads["low"].wait()
+    change = low[2] * times_t(y1, sl[5]) + low[4] * times_t(y2, sl[7])
+
+    def between_b():
+        loads["e0"].wait()
+        return low[1] * times_t(y1, sl[4]) + low[3] * times_t(y2, sl[6])
+
+    (change,), to_anc = swap(1, [change], row_list, one_send.at[0], one_recv.at[0], between_b)
+    r0 = (given0 - change).astype(BF)
+    (y0,), unused = swap(2, [times(r0, sl[0])], col_list, one_send.at[1], one_recv.at[1])
+    y0 = y0.astype(BF)
+
+    to_anc = to_anc + low[0] * times_t(y0, sl[3])
+    (reached,), unused = swap(3, [to_anc], wide, all_send, all_recv)
+    ra = (given_anc - reached).astype(BF)
+    loads["al"].wait()
+    part = times(ra, al[0])
+
+    one_send[2, 0] = part.astype(BF)
+
+    @pl.when(row != col)
+    def to_diag():
+        slot = lax.rem(col - row + cols_n - 1, cols_n)
+        copy = pltpu.make_async_remote_copy(
+            src_ref=one_send.at[2],
+            dst_ref=one_recv.at[2, slot],
+            send_sem=send_sem.at[4, 0],
+            recv_sem=recv_sem.at[4, slot],
+            device_id=(gz, row, row),
+            device_id_type=MESH,
+        )
+        copy.start()
+        copy.wait_send()
+
+    spread = [
+        pltpu.make_async_remote_copy(
+            src_ref=one_send.at[3],
+            dst_ref=diag_recv,
+            send_sem=send_sem.at[5, j],
+            recv_sem=recv_sem.at[5, 0],
+            device_id=peer,
+            device_id_type=MESH,
+        )
+        for j, peer in enumerate(row_list)
+    ]
+
+    @pl.when(row == col)
+    def at_diag():
+        total = part
+        for j in range(cols_n - 1):
+            pltpu.make_async_remote_copy(
+                src_ref=one_send.at[2],
+                dst_ref=one_recv.at[2, j],
+                send_sem=send_sem.at[4, 0],
+                recv_sem=recv_sem.at[4, j],
+                device_id=(gz, row, col),
+                device_id_type=MESH,
+            ).wait_recv()
+            total = total + one_recv[2, j, 0].astype(F32)
+        one_send[3, 0] = total.astype(BF)
+        for copy in spread:
+            copy.start()
+        diag_recv[0] = total.astype(BF)
+        for copy in spread:
+            copy.wait_send()
+
+    @pl.when(row != col)
+    def off_diag():
+        spread[0].wait_recv()
+
+    ta = diag_recv[0]
+
+    loads["au"].wait()
+    loads["su"].wait()
+    (za_full,), unused = swap(6, [times(ta, au[0])], col_list, one_send.at[4], one_recv.at[4])
+    za = za_full.astype(BF)
+    piece = za_full.shape[1] // cols_n
+    mine = pl.ds(pl.multiple_of(col * piece, piece), piece)
+
+    part = on_diag * y0.astype(F32) - up[0] * times_t(za, su[3])
+
+    def between_i():
+        flipped[0] = jnp.transpose(za_full)
+        anc_out[0] = flipped[0, mine, :]
+        return (
+            on_diag * y1.astype(F32) - up[1] * times_t(za, su[4]),
+            on_diag * y2.astype(F32) - up[3] * times_t(za, su[6]),
+        )
+
+    (t0,), (s1, s2) = swap(7, [part], row_list, one_send.at[5], one_recv.at[5], between_i)
+    (z0_full,), unused = swap(
+        8, [times(t0.astype(BF), su[0])], col_list, one_send.at[6], one_recv.at[6]
+    )
+    z0 = z0_full.astype(BF)
+
+    s1 = s1 - up[2] * times_t(z0, su[5])
+    s2 = s2 - up[4] * times_t(z0, su[7])
+
+    def between_k():
+        flipped[1] = jnp.transpose(z0_full)
+        sub_out[0] = flipped[1, mine, :]
+
+    (t1, t2), unused = swap(9, [s1, s2], row_list, pair_send.at[1], pair_recv.at[1], between_k)
+    part1 = times(t1.astype(BF), su[1])
+    part2 = times(t2.astype(BF), su[2])
+    for c in range(cols_n):
+        lanes = slice(c * piece, (c + 1) * piece)
+        piece_send[c] = jnp.concatenate([part1[:, lanes], part2[:, lanes]], 1).astype(BF)
+    made = send(
+        10,
+        lambda j: piece_send.at[lax.rem(col + j + 1, cols_n)],
+        lambda j: piece_recv.at[j],
+        col_list,
+    )
+    total = piece_send[col].astype(F32)
+    for j, copy in enumerate(made):
+        copy.wait_recv()
+        total = total + piece_recv[j].astype(F32)
+    total = jnp.transpose(total)
+    sub_out[1] = total[:piece]
+    sub_out[2] = total[piece:]
+    for copy in started:
+        copy.wait_send()
+
+
+def fused(mesh):
+    layers, rows_n, cols_n = (mesh.shape[a] for a in ("gz", "row", "col"))
+
+    def local_fused(*args):
+        anc_lower, anc_upper, sub_lower, sub_upper, anc_rhs, sub_rhs, subtree, pattern = args
+        cut, right = anc_rhs.shape[1], anc_rhs.shape[2]
+        piece = cut // cols_n
+        vec = (right, cut)
+        peers_n = max(rows_n, cols_n) - 1
+        hbm = pl.BlockSpec(memory_space=pl.ANY)
+        smem = pl.BlockSpec(memory_space=pltpu.SMEM)
+        vmem = pl.BlockSpec(memory_space=pltpu.VMEM)
+        return pl.pallas_call(
+            functools.partial(fused_kernel, layers, rows_n, cols_n),
+            out_shape=(
+                jax.ShapeDtypeStruct((1, piece, right), F32),
+                jax.ShapeDtypeStruct((SUB_NODES, piece, right), F32),
+            ),
+            in_specs=[hbm] * 6 + [smem] * 2,
+            out_specs=(vmem, vmem),
+            scratch_shapes=[
+                pltpu.VMEM(anc_lower.shape, BF),
+                pltpu.VMEM(anc_upper.shape, BF),
+                pltpu.VMEM(sub_lower.shape, BF),
+                pltpu.VMEM(sub_upper.shape, BF),
+                pltpu.VMEM(anc_rhs.shape, BF),
+                pltpu.VMEM(sub_rhs.shape, BF),
+                pltpu.VMEM((2, 2) + vec, BF),
+                pltpu.VMEM((2, peers_n, 2) + vec, BF),
+                pltpu.VMEM((7, 1) + vec, BF),
+                pltpu.VMEM((7, peers_n, 1) + vec, BF),
+                pltpu.VMEM((1,) + vec, BF),
+                pltpu.VMEM((layers * rows_n - 1, 1) + vec, BF),
+                pltpu.VMEM((1,) + vec, BF),
+                pltpu.VMEM((2, cut, right), F32),
+                pltpu.VMEM((cols_n, right, 2 * piece), BF),
+                pltpu.VMEM((cols_n - 1, right, 2 * piece), BF),
+                pltpu.SemaphoreType.DMA((8,)),
+                pltpu.SemaphoreType.DMA((11, layers * rows_n)),
+                pltpu.SemaphoreType.DMA((11, layers * rows_n)),
+            ],
+            compiler_params=pltpu.CompilerParams(collective_id=0, has_side_effects=True),
+        )(*args)
+
+    return local_fused
+
+
 def solution(mesh):
     in_specs = (
         P(None, "col", "row"),
@@ -201,4 +522,7 @@
         P("gz", None),
     )
     out_specs = (P(None, ("row", "col"), None), P("gz", ("row", "col"), None))
-    return jax.shard_map(local, mesh=mesh, in_specs=in_specs, out_specs=out_specs, check_vma=False)
+    one_anc = mesh.shape["gz"] == 2
+    square = mesh.shape["row"] == mesh.shape["col"] == 4
+    body = fused(mesh) if one_anc and square else local
+    return jax.shard_map(body, mesh=mesh, in_specs=in_specs, out_specs=out_specs, check_vma=False)

time: 253 us -> 62.8 us (0.25)
  blocking collectives: 188 us -> 0 us
  Pallas kernels: 0 us -> 55.2 us
  waiting for transfers between devices: 32.9 us -> 0 us
  between operations: 14.7 us -> 0.65 us
  matrix products: 6.59 us -> 0 us
    all_gather x10 -> x0, blocking collectives: 154 us -> none  [the longest x6 85.3 us: solve_diagonal(): whole_res = lax.all_gather(residual, 'col', axis=1, tiled=True)]
    pallas_call x0 -> x1, Pallas kernels: none -> 55.2 us  [local_fused(): pl.pallas_call(functools.partial(fused_kernel, layers, rows_n, cols_n), o...]
    psum x3 -> x0, blocking collectives: 34 us -> none  [upper_sum(): return lax.psum(values, 'row')]
    psum x2 -> x0, waiting for transfers between devices: 32.8 us -> none  [the longest x1 30 us: local(): given = given - lax.psum(sub_acc[first_id:stop_id], 'row')]
    dot_general x12 -> x0, matrix products: 6.59 us -> none  [the longest x6 3.94 us: solve_diagonal(): jnp.einsum('nki,nkr->nir', whole_blocks, whole_res, preferred_element_typ...]
    slice x15 -> x0, local copies, waits for them, and re-layouts: 2.63 us -> none  [the longest x3 1.68 us: local(): sub_lower[first_id:stop_id]]
    unnamed x20 -> x7, local copies, waits for them, and re-layouts: 3.97 us -> 6.59 us
  transfers between devices with their start and end apart: 4 -> 0, of which waited for: 2 -> 0; matrix products, arithmetic and copies ran while one was open for 2% -> 0% of each run, Pallas kernels for 0% -> 0%
where the time goes in v1:
time: 62.8 us; the launch traced here: 62.4 us
  Pallas kernels  55.2 us (88%)
  local copies, waits for them, and re-layouts  6.59 us (10%)
  between operations  0.65 us (1%)
    pallas_call x1, Pallas kernels, local_fused(): pl.pallas_call(functools.partial(fused_kernel, layers, rows_n, cols_n), o...  55.2 us
    unnamed x7, local copies, waits for them, and re-layouts  6.59 us

profile of v1, /device:TPU:0, one launch (start us, length us, event | category | flops | bytes accessed | tf_op | source)
XLA Modules:
  0.0 62.4 jit_solution(6343540187899874720)
XLA Ops:
  0.6 0.0 copy-start
  0.6 1.4 %copy.12.pattern = s32[5,2]{1,0:T(8,128)} copy(s32[5,2]{0,1:T(2,128)} %param.15) | data formatting | bytes 80 | tf_op args[7]
  2.0 1.5 %copy.10.anc_rhs = bf16[1,256,64]{2,1,0:T(8,128)(2,1)} copy(bf16[1,256,64]{1,2,0:T(8,128)(2,1)} %param.12) | data formatting | bytes 65536 | tf_op args[4]
  3.5 0.0 copy-done
  3.5 0.8 %copy.11.sub_rhs = bf16[3,256,64]{2,1,0:T(8,128)(2,1)} copy(bf16[3,256,64]{1,2,0:T(8,128)(2,1)S(1)} %copy-done) | data formatting | bytes 196608 | tf_op args[5]
  4.3 55.2 %shard_map.95 = (f32[1,64,64]{2,1,0:T(8,128)}, f32[3,64,64]{2,1,0:T(8,128)}) custom-call(bf16[1,256,256]{2,1,0:T(8,128)(2,1)} %anc_lower.1, bf16[1,256,256]{2,1,0:T(8,128)(2,1)} %anc_upper.1, bf16[8,256,256]{2,1,0:T(8,128)(2,1)} %sub_lower.1, bf16[8,256,256]{2,1,0:T(8,128)(2,1)} %sub_upper.1, bf16[1,256,64]{2,1,0:T(8,128)(2,1)} %copy.10.anc_rhs, ...), custom_call_target="tpu_custom_call" | custom-call | tf_op jit(solution)/shard_map/pallas_call | solution.py:478
  59.5 1.4 %copy.15 = f32[1,64,64]{2,1,0:T(8,128)} copy(f32[1,64,64]{2,1,0:T(8,128)} %get-tuple-element.4) | data formatting | bytes 32768
  60.9 1.5 %copy.16 = f32[3,64,64]{2,1,0:T(8,128)} copy(f32[3,64,64]{2,1,0:T(8,128)} %get-tuple-element.5) | data formatting | bytes 98304
Async XLA Ops:
  0.6 2.9 %copy-start = (bf16[3,256,64]{1,2,0:T(8,128)(2,1)S(1)}, bf16[3,256,64]{1,2,0:T(8,128)(2,1)}, u32[]{:S(2)}) copy-start(bf16[3,256,64]{1,2,0:T(8,128)(2,1)} %param.13) | copy-start | bytes 294916

commit v2 on v1

--- a/solution.py
+++ b/solution.py
@@ -196,6 +196,7 @@
 BF = jnp.bfloat16
 F32 = jnp.float32
 MESH = pl.DeviceIdType.MESH
+HALVES = 2
 
 
 def times(vectors, block):
@@ -204,10 +205,6 @@
 
 def times_t(vectors, block):
     return lax.dot_general(vectors, block, (((1,), (1,)), ((), ())), preferred_element_type=F32)
-
-
-def flip(rows):
-    return jnp.transpose(rows.astype(F32))
 
 
 def fused_kernel(
@@ -282,15 +279,18 @@
         pl.semaphore_signal(barrier, inc=1, device_id=peer, device_id_type=MESH)
 
     started = []
-
-    def send(step, source, target, peer_list):
+    half = sr.shape[1] // HALVES
+    span = [slice(h * half, (h + 1) * half) for h in range(HALVES)]
+    each = range(HALVES)
+
+    def send(h, step, source, target, peer_list):
         made = []
         for j, peer in enumerate(peer_list):
             copy = pltpu.make_async_remote_copy(
                 src_ref=source(j),
                 dst_ref=target(j),
-                send_sem=send_sem.at[step, j],
-                recv_sem=recv_sem.at[step, j],
+                send_sem=send_sem.at[h, step, j],
+                recv_sem=recv_sem.at[h, step, j],
                 device_id=peer,
                 device_id_type=MESH,
             )
@@ -299,164 +299,195 @@
         started.extend(made)
         return made
 
-    def swap(step, values, peer_list, send_buf, recv_buf, between=None):
+    def begin(h, step, values, peer_list, send_buf, recv_buf):
         for n, value in enumerate(values):
-            send_buf[n] = value.astype(BF)
-        made = send(step, lambda j: send_buf, lambda j: recv_buf.at[j], peer_list)
-        extra = between() if between is not None else None
-        sums = list(values)
+            send_buf[h, n] = value.astype(BF)
+        made = send(h, step, lambda j: send_buf.at[h], lambda j: recv_buf.at[h, j], peer_list)
+        return h, list(values), made, recv_buf
+
+    def finish(handle):
+        h, sums, made, recv_buf = handle
         for j, copy in enumerate(made):
             copy.wait_recv()
             for n in range(len(sums)):
-                sums[n] = sums[n] + recv_buf[j, n].astype(F32)
-        return sums, extra
+                sums[n] = sums[n] + recv_buf[h, j, n].astype(F32)
+        return sums
 
     row_list = [row_peer(j) for j in range(1, rows_n)]
     col_list = [col_peer(j) for j in range(1, cols_n)]
 
     anc_here = jnp.where((layers + layer_subtree[gz]) // layers - 1 == 0, 1, 0)
-    low = [pattern[p, 0] for p in range(5)]
-    up = [pattern[p, 1] for p in range(5)]
+    low = [pattern[0, p] for p in range(5)]
+    up = [pattern[1, p] for p in range(5)]
     low = [(w * anc_here if p in (0, 1, 3) else w).astype(F32) for p, w in enumerate(low)]
     up = [(w * anc_here if p in (0, 1, 3) else w).astype(F32) for p, w in enumerate(up)]
     on_diag = jnp.where(row == col, 1.0, 0.0).astype(F32)
 
     loads["sr"].wait()
-    r1 = flip(sr[1]).astype(BF)
-    r2 = flip(sr[2]).astype(BF)
     loads["e12"].wait()
-    part1 = times(r1, sl[1])
-    part2 = times(r2, sl[2])
+    parts = [[times(sr[m, span[h]], sl[m]) for m in (1, 2)] for h in each]
     pl.semaphore_wait(barrier, len(peers))
-
-    def between_a():
-        loads["ar"].wait()
-        return flip(sr[0]), flip(ar[0])
-
-    (y1, y2), (given0, given_anc) = swap(
-        0, [part1, part2], col_list, pair_send.at[0], pair_recv.at[0], between_a
-    )
-    y1 = y1.astype(BF)
-    y2 = y2.astype(BF)
+    step = [begin(h, 0, parts[h], col_list, pair_send.at[0], pair_recv.at[0]) for h in each]
     loads["low"].wait()
-    change = low[2] * times_t(y1, sl[5]) + low[4] * times_t(y2, sl[7])
-
-    def between_b():
-        loads["e0"].wait()
-        return low[1] * times_t(y1, sl[4]) + low[3] * times_t(y2, sl[6])
-
-    (change,), to_anc = swap(1, [change], row_list, one_send.at[0], one_recv.at[0], between_b)
-    r0 = (given0 - change).astype(BF)
-    (y0,), unused = swap(2, [times(r0, sl[0])], col_list, one_send.at[1], one_recv.at[1])
-    y0 = y0.astype(BF)
-
-    to_anc = to_anc + low[0] * times_t(y0, sl[3])
-    (reached,), unused = swap(3, [to_anc], wide, all_send, all_recv)
-    ra = (given_anc - reached).astype(BF)
+    y = [None] * HALVES
+    for h in each:
+        y[h] = [v.astype(BF) for v in finish(step[h])]
+        change = low[2] * times_t(y[h][0], sl[5]) + low[4] * times_t(y[h][1], sl[7])
+        step[h] = begin(h, 1, [change], row_list, one_send.at[0], one_recv.at[0])
+    loads["e0"].wait()
+    to_anc = [low[1] * times_t(y[h][0], sl[4]) + low[3] * times_t(y[h][1], sl[6]) for h in each]
+
+    for h in each:
+        r0 = (sr[0, span[h]].astype(F32) - finish(step[h])[0]).astype(BF)
+        step[h] = begin(h, 2, [times(r0, sl[0])], col_list, one_send.at[1], one_recv.at[1])
+    loads["ar"].wait()
     loads["al"].wait()
-    part = times(ra, al[0])
-
-    one_send[2, 0] = part.astype(BF)
-
-    @pl.when(row != col)
-    def to_diag():
-        slot = lax.rem(col - row + cols_n - 1, cols_n)
-        copy = pltpu.make_async_remote_copy(
-            src_ref=one_send.at[2],
-            dst_ref=one_recv.at[2, slot],
-            send_sem=send_sem.at[4, 0],
-            recv_sem=recv_sem.at[4, slot],
-            device_id=(gz, row, row),
-            device_id_type=MESH,
-        )
-        copy.start()
-        copy.wait_send()
-
-    spread = [
-        pltpu.make_async_remote_copy(
-            src_ref=one_send.at[3],
-            dst_ref=diag_recv,
-            send_sem=send_sem.at[5, j],
-            recv_sem=recv_sem.at[5, 0],
-            device_id=peer,
-            device_id_type=MESH,
-        )
-        for j, peer in enumerate(row_list)
-    ]
-
-    @pl.when(row == col)
-    def at_diag():
-        total = part
-        for j in range(cols_n - 1):
+    for h in each:
+        y0 = finish(step[h])[0].astype(BF)
+        y[h] = [y0] + y[h]
+        step[h] = begin(
+            h, 3, [to_anc[h] + low[0] * times_t(y0, sl[3])], wide, all_send, all_recv
+        )
+
+    for h in each:
+        ra = (ar[0, span[h]].astype(F32) - finish(step[h])[0]).astype(BF)
+        part = times(ra, al[0])
+        step[h] = part
+        one_send[2, h, 0] = part.astype(BF)
+
+        @pl.when(row != col)
+        def to_diag():
+            slot = lax.rem(col - row + cols_n - 1, cols_n)
+            copy = pltpu.make_async_remote_copy(
+                src_ref=one_send.at[2, h],
+                dst_ref=one_recv.at[2, h, slot],
+                send_sem=send_sem.at[h, 4, 0],
+                recv_sem=recv_sem.at[h, 4, slot],
+                device_id=(gz, row, row),
+                device_id_type=MESH,
+            )
+            copy.start()
+
+    for h in each:
+        spread = [
             pltpu.make_async_remote_copy(
-                src_ref=one_send.at[2],
-                dst_ref=one_recv.at[2, j],
-                send_sem=send_sem.at[4, 0],
-                recv_sem=recv_sem.at[4, j],
-                device_id=(gz, row, col),
+                src_ref=one_send.at[3, h],
+                dst_ref=diag_recv.at[h],
+                send_sem=send_sem.at[h, 5, j],
+                recv_sem=recv_sem.at[h, 5, 0],
+                device_id=peer,
                 device_id_type=MESH,
-            ).wait_recv()
-            total = total + one_recv[2, j, 0].astype(F32)
-        one_send[3, 0] = total.astype(BF)
-        for copy in spread:
-            copy.start()
-        diag_recv[0] = total.astype(BF)
-        for copy in spread:
-            copy.wait_send()
-
-    @pl.when(row != col)
-    def off_diag():
-        spread[0].wait_recv()
-
-    ta = diag_recv[0]
+            )
+            for j, peer in enumerate(row_list)
+        ]
+
+        @pl.when(row == col)
+        def at_diag():
+            total = step[h]
+            for j in range(cols_n - 1):
+                pltpu.make_async_remote_copy(
+                    src_ref=one_send.at[2, h],
+                    dst_ref=one_recv.at[2, h, j],
+                    send_sem=send_sem.at[h, 4, 0],
+                    recv_sem=recv_sem.at[h, 4, j],
+                    device_id=(gz, row, col),
+                    device_id_type=MESH,
+                ).wait_recv()
+                total = total + one_recv[2, h, j, 0].astype(F32)
+            one_send[3, h, 0] = total.astype(BF)
+            for copy in spread:
+                copy.start()
+            diag_recv[h, 0] = total.astype(BF)
 
     loads["au"].wait()
     loads["su"].wait()
-    (za_full,), unused = swap(6, [times(ta, au[0])], col_list, one_send.at[4], one_recv.at[4])
-    za = za_full.astype(BF)
-    piece = za_full.shape[1] // cols_n
+    for h in each:
+        spread = [
+            pltpu.make_async_remote_copy(
+                src_ref=one_send.at[3, h],
+                dst_ref=diag_recv.at[h],
+                send_sem=send_sem.at[h, 5, j],
+                recv_sem=recv_sem.at[h, 5, 0],
+                device_id=peer,
+                device_id_type=MESH,
+            )
+            for j, peer in enumerate(row_list)
+        ]
+
+        @pl.when(row == col)
+        def sent_diag():
+            for copy in spread:
+                copy.wait_send()
+
+        @pl.when(row != col)
+        def off_diag():
+            pltpu.make_async_remote_copy(
+                src_ref=one_send.at[2, h],
+                dst_ref=one_recv.at[2, h, 0],
+                send_sem=send_sem.at[h, 4, 0],
+                recv_sem=recv_sem.at[h, 4, 0],
+                device_id=(gz, row, row),
+                device_id_type=MESH,
+            ).wait_send()
+            spread[0].wait_recv()
+
+        part = times(diag_recv[h, 0], au[0])
+        step[h] = begin(h, 6, [part], col_list, one_send.at[4], one_recv.at[4])
+    piece = sr.shape[2] // cols_n
     mine = pl.ds(pl.multiple_of(col * piece, piece), piece)
 
-    part = on_diag * y0.astype(F32) - up[0] * times_t(za, su[3])
-
-    def between_i():
-        flipped[0] = jnp.transpose(za_full)
-        anc_out[0] = flipped[0, mine, :]
-        return (
-            on_diag * y1.astype(F32) - up[1] * times_t(za, su[4]),
-            on_diag * y2.astype(F32) - up[3] * times_t(za, su[6]),
-        )
-
-    (t0,), (s1, s2) = swap(7, [part], row_list, one_send.at[5], one_recv.at[5], between_i)
-    (z0_full,), unused = swap(
-        8, [times(t0.astype(BF), su[0])], col_list, one_send.at[6], one_recv.at[6]
-    )
-    z0 = z0_full.astype(BF)
-
-    s1 = s1 - up[2] * times_t(z0, su[5])
-    s2 = s2 - up[4] * times_t(z0, su[7])
-
-    def between_k():
-        flipped[1] = jnp.transpose(z0_full)
-        sub_out[0] = flipped[1, mine, :]
-
-    (t1, t2), unused = swap(9, [s1, s2], row_list, pair_send.at[1], pair_recv.at[1], between_k)
-    part1 = times(t1.astype(BF), su[1])
-    part2 = times(t2.astype(BF), su[2])
-    for c in range(cols_n):
-        lanes = slice(c * piece, (c + 1) * piece)
-        piece_send[c] = jnp.concatenate([part1[:, lanes], part2[:, lanes]], 1).astype(BF)
-    made = send(
-        10,
-        lambda j: piece_send.at[lax.rem(col + j + 1, cols_n)],
-        lambda j: piece_recv.at[j],
-        col_list,
-    )
-    total = piece_send[col].astype(F32)
-    for j, copy in enumerate(made):
-        copy.wait_recv()
-        total = total + piece_recv[j].astype(F32)
-    total = jnp.transpose(total)
+    za_full = [None] * HALVES
+    za = [None] * HALVES
+    for h in each:
+        za_full[h] = finish(step[h])[0]
+        za[h] = za_full[h].astype(BF)
+        part = on_diag * y[h][0].astype(F32) - up[0] * times_t(za[h], su[3])
+        step[h] = begin(h, 7, [part], row_list, one_send.at[5], one_recv.at[5])
+    left = [
+        [
+            on_diag * y[h][1].astype(F32) - up[1] * times_t(za[h], su[4]),
+            on_diag * y[h][2].astype(F32) - up[3] * times_t(za[h], su[6]),
+        ]
+        for h in each
+    ]
+    flipped[0] = jnp.transpose(jnp.concatenate(za_full, 0))
+    anc_out[0] = flipped[0, mine, :]
+    for h in each:
+        t0 = finish(step[h])[0].astype(BF)
+        step[h] = begin(h, 8, [times(t0, su[0])], col_list, one_send.at[6], one_recv.at[6])
+
+    z0_full = [None] * HALVES
+    for h in each:
+        z0_full[h] = finish(step[h])[0]
+        z0 = z0_full[h].astype(BF)
+        s1 = left[h][0] - up[2] * times_t(z0, su[5])
+        s2 = left[h][1] - up[4] * times_t(z0, su[7])
+        step[h] = begin(h, 9, [s1, s2], row_list, pair_send.at[1], pair_recv.at[1])
+    flipped[1] = jnp.transpose(jnp.concatenate(z0_full, 0))
+    sub_out[0] = flipped[1, mine, :]
+    for h in each:
+        t1, t2 = finish(step[h])
+        part1 = times(t1.astype(BF), su[1])
+        part2 = times(t2.astype(BF), su[2])
+        for c in range(cols_n):
+            lanes = slice(c * piece, (c + 1) * piece)
+            both = jnp.concatenate([part1[:, lanes], part2[:, lanes]], 1)
+            piece_send[h, c] = both.astype(BF)
+        step[h] = send(
+            h,
+            10,
+            lambda j: piece_send.at[h, lax.rem(col + j + 1, cols_n)],
+            lambda j: piece_recv.at[h, j],
+            col_list,
+        )
+    totals = []
+    for h in each:
+        total = piece_send[h, col].astype(F32)
+        for j, copy in enumerate(step[h]):
+            copy.wait_recv()
+            total = total + piece_recv[h, j].astype(F32)
+        totals.append(total)
+    total = jnp.transpose(jnp.concatenate(totals, 0))
     sub_out[1] = total[:piece]
     sub_out[2] = total[piece:]
     for copy in started:
@@ -469,8 +500,13 @@
     def local_fused(*args):
         anc_lower, anc_upper, sub_lower, sub_upper, anc_rhs, sub_rhs, subtree, pattern = args
         cut, right = anc_rhs.shape[1], anc_rhs.shape[2]
+        anc_rhs = jnp.swapaxes(anc_rhs, 1, 2)
+        sub_rhs = jnp.swapaxes(sub_rhs, 1, 2)
+        pattern = jnp.swapaxes(pattern, 0, 1)
+        args = args[:4] + (anc_rhs, sub_rhs, subtree, pattern)
         piece = cut // cols_n
-        vec = (right, cut)
+        vec = (right // HALVES, cut)
+        H = HALVES
         peers_n = max(rows_n, cols_n) - 1
         hbm = pl.BlockSpec(memory_space=pl.ANY)
         smem = pl.BlockSpec(memory_space=pltpu.SMEM)
@@ -490,19 +526,19 @@
                 pltpu.VMEM(sub_upper.shape, BF),
                 pltpu.VMEM(anc_rhs.shape, BF),
                 pltpu.VMEM(sub_rhs.shape, BF),
-                pltpu.VMEM((2, 2) + vec, BF),
-                pltpu.VMEM((2, peers_n, 2) + vec, BF),
-                pltpu.VMEM((7, 1) + vec, BF),
-                pltpu.VMEM((7, peers_n, 1) + vec, BF),
-                pltpu.VMEM((1,) + vec, BF),
-                pltpu.VMEM((layers * rows_n - 1, 1) + vec, BF),
-                pltpu.VMEM((1,) + vec, BF),
+                pltpu.VMEM((2, H, 2) + vec, BF),
+                pltpu.VMEM((2, H, peers_n, 2) + vec, BF),
+                pltpu.VMEM((7, H, 1) + vec, BF),
+                pltpu.VMEM((7, H, peers_n, 1) + vec, BF),
+                pltpu.VMEM((H, 1) + vec, BF),
+                pltpu.VMEM((H, layers * rows_n - 1, 1) + vec, BF),
+                pltpu.VMEM((H, 1) + vec, BF),
                 pltpu.VMEM((2, cut, right), F32),
-                pltpu.VMEM((cols_n, right, 2 * piece), BF),
-                pltpu.VMEM((cols_n - 1, right, 2 * piece), BF),
+                pltpu.VMEM((H, cols_n, right // H, 2 * piece), BF),
+                pltpu.VMEM((H, cols_n - 1, right // H, 2 * piece), BF),
                 pltpu.SemaphoreType.DMA((8,)),
-                pltpu.SemaphoreType.DMA((11, layers * rows_n)),
-                pltpu.SemaphoreType.DMA((11, layers * rows_n)),
+                pltpu.SemaphoreType.DMA((H, 11, layers * rows_n)),
+                pltpu.SemaphoreType.DMA((H, 11, layers * rows_n)),
             ],
             compiler_params=pltpu.CompilerParams(collective_id=0, has_side_effects=True),
         )(*args)

time: 62.8 us -> 56.8 us (0.904)
  local copies, waits for them, and re-layouts: 6.59 us -> 2.91 us
  Pallas kernels: 55.2 us -> 53 us
    unnamed x7 -> x2, local copies, waits for them, and re-layouts: 6.59 us -> 2.91 us
    pallas_call x1, Pallas kernels: 55.2 us -> 53 us  [local_fused(): pl.pallas_call(functools.partial(fused_kernel, layers, rows_n, cols_n), o...]
where the time goes in v2:
time: 56.8 us; the launch traced here: 56.6 us
  Pallas kernels  53 us (93%)
  local copies, waits for them, and re-layouts  2.91 us (5%)
  between operations  0.64 us (1%)
    pallas_call x1, Pallas kernels, local_fused(): pl.pallas_call(functools.partial(fused_kernel, layers, rows_n, cols_n), o...  53 us
    unnamed x2, local copies, waits for them, and re-layouts  2.91 us

profile of v2, /device:TPU:0, one launch (start us, length us, event | category | flops | bytes accessed | tf_op | source)
XLA Modules:
  0.0 56.6 jit_solution(2732793779594067394)
XLA Ops:
  0.6 53.0 %shard_map.95 = (f32[1,64,64]{2,1,0:T(8,128)}, f32[3,64,64]{2,1,0:T(8,128)}) custom-call(bf16[1,256,256]{2,1,0:T(8,128)(2,1)} %anc_lower.1, bf16[1,256,256]{2,1,0:T(8,128)(2,1)} %anc_upper.1, bf16[8,256,256]{2,1,0:T(8,128)(2,1)} %sub_lower.1, bf16[8,256,256]{2,1,0:T(8,128)(2,1)} %sub_upper.1, bf16[1,64,256]{2,1,0:T(8,128)(2,1)} %bitcast.4, ...), custom_call_target="tpu_custom_call" | custom-call | tf_op jit(solution)/shard_map/pallas_call | solution.py:514
  53.7 1.4 %copy.12 = f32[1,64,64]{2,1,0:T(8,128)} copy(f32[1,64,64]{2,1,0:T(8,128)} %get-tuple-element.4) | data formatting | bytes 32768
  55.0 1.5 %copy.13 = f32[3,64,64]{2,1,0:T(8,128)} copy(f32[3,64,64]{2,1,0:T(8,128)} %get-tuple-element.5) | data formatting | bytes 98304

commit v3 on v2

--- a/solution.py
+++ b/solution.py
@@ -233,7 +233,8 @@
     one_recv,
     all_send,
     all_recv,
-    diag_recv,
+    product_send,
+    product_recv,
     flipped,
     piece_send,
     piece_recv,
@@ -256,8 +257,13 @@
     load("low", sub_lower.at[pl.ds(3, 5)], sl.at[pl.ds(3, 5)])
     load("e0", sub_lower.at[0], sl.at[0])
     load("ar", anc_rhs, ar)
-    load("al", anc_lower, al)
-    load("au", anc_upper, au)
+    width = au.shape[2]
+    load("al", anc_lower, al.at[pl.ds(0, 1)])
+    load(
+        "au",
+        anc_upper.at[:, :, pl.ds(pl.multiple_of(gz * width, width), width)],
+        au.at[pl.ds(0, 1)],
+    )
     load("su", sub_upper, su)
 
     def row_peer(j):
@@ -328,6 +334,11 @@
     parts = [[times(sr[m, span[h]], sl[m]) for m in (1, 2)] for h in each]
     pl.semaphore_wait(barrier, len(peers))
     step = [begin(h, 0, parts[h], col_list, pair_send.at[0], pair_recv.at[0]) for h in each]
+
+    loads["al"].wait()
+    loads["au"].wait()
+    blocks = send(0, 4, lambda j: al.at[0], lambda j: al.at[j + 1], row_list)
+    blocks = blocks + send(0, 5, lambda j: au.at[0], lambda j: au.at[j + 1], col_list)
     loads["low"].wait()
     y = [None] * HALVES
     for h in each:
@@ -341,7 +352,19 @@
         r0 = (sr[0, span[h]].astype(F32) - finish(step[h])[0]).astype(BF)
         step[h] = begin(h, 2, [times(r0, sl[0])], col_list, one_send.at[1], one_recv.at[1])
     loads["ar"].wait()
-    loads["al"].wait()
+    for copy in blocks:
+        copy.wait_recv()
+    product = jnp.zeros((al.shape[1], width), F32)
+    for b in range(rows_n):
+        product = product + times(
+            al[lax.rem(row - b + rows_n, rows_n)], au[lax.rem(col - b + cols_n, cols_n)]
+        )
+    product_send[0] = product.astype(BF)
+    product_recv[0] = product.astype(BF)
+    layer_list = [(lax.rem(gz + g, layers), row, col) for g in range(1, layers)]
+    blocks = send(
+        0, 11, lambda j: product_send.at[0], lambda j: product_recv.at[j + 1], layer_list
+    )
     for h in each:
         y0 = finish(step[h])[0].astype(BF)
         y[h] = [y0] + y[h]
@@ -349,90 +372,15 @@
             h, 3, [to_anc[h] + low[0] * times_t(y0, sl[3])], wide, all_send, all_recv
         )
 
+    for copy in blocks:
+        copy.wait_recv()
+    whole = jnp.concatenate(
+        [product_recv[lax.rem(gz - g + layers, layers)] for g in range(layers)], 1
+    )
     for h in each:
         ra = (ar[0, span[h]].astype(F32) - finish(step[h])[0]).astype(BF)
-        part = times(ra, al[0])
-        step[h] = part
-        one_send[2, h, 0] = part.astype(BF)
-
-        @pl.when(row != col)
-        def to_diag():
-            slot = lax.rem(col - row + cols_n - 1, cols_n)
-            copy = pltpu.make_async_remote_copy(
-                src_ref=one_send.at[2, h],
-                dst_ref=one_recv.at[2, h, slot],
-                send_sem=send_sem.at[h, 4, 0],
-                recv_sem=recv_sem.at[h, 4, slot],
-                device_id=(gz, row, row),
-                device_id_type=MESH,
-            )
-            copy.start()
-
-    for h in each:
-        spread = [
-            pltpu.make_async_remote_copy(
-                src_ref=one_send.at[3, h],
-                dst_ref=diag_recv.at[h],
-                send_sem=send_sem.at[h, 5, j],
-                recv_sem=recv_sem.at[h, 5, 0],
-                device_id=peer,
-                device_id_type=MESH,
-            )
-            for j, peer in enumerate(row_list)
-        ]
-
-        @pl.when(row == col)
-        def at_diag():
-            total = step[h]
-            for j in range(cols_n - 1):
-                pltpu.make_async_remote_copy(
-                    src_ref=one_send.at[2, h],
-                    dst_ref=one_recv.at[2, h, j],
-                    send_sem=send_sem.at[h, 4, 0],
-                    recv_sem=recv_sem.at[h, 4, j],
-                    device_id=(gz, row, col),
-                    device_id_type=MESH,
-                ).wait_recv()
-                total = total + one_recv[2, h, j, 0].astype(F32)
-            one_send[3, h, 0] = total.astype(BF)
-            for copy in spread:
-                copy.start()
-            diag_recv[h, 0] = total.astype(BF)
-
-    loads["au"].wait()
+        step[h] = begin(h, 6, [times(ra, whole)], col_list, one_send.at[4], one_recv.at[4])
     loads["su"].wait()
-    for h in each:
-        spread = [
-            pltpu.make_async_remote_copy(
-                src_ref=one_send.at[3, h],
-                dst_ref=diag_recv.at[h],
-                send_sem=send_sem.at[h, 5, j],
-                recv_sem=recv_sem.at[h, 5, 0],
-                device_id=peer,
-                device_id_type=MESH,
-            )
-            for j, peer in enumerate(row_list)
-        ]
-
-        @pl.when(row == col)
-        def sent_diag():
-            for copy in spread:
-                copy.wait_send()
-
-        @pl.when(row != col)
-        def off_diag():
-            pltpu.make_async_remote_copy(
-                src_ref=one_send.at[2, h],
-                dst_ref=one_recv.at[2, h, 0],
-                send_sem=send_sem.at[h, 4, 0],
-                recv_sem=recv_sem.at[h, 4, 0],
-                device_id=(gz, row, row),
-                device_id_type=MESH,
-            ).wait_send()
-            spread[0].wait_recv()
-
-        part = times(diag_recv[h, 0], au[0])
-        step[h] = begin(h, 6, [part], col_list, one_send.at[4], one_recv.at[4])
     piece = sr.shape[2] // cols_n
     mine = pl.ds(pl.multiple_of(col * piece, piece), piece)
 
@@ -514,14 +462,14 @@
         return pl.pallas_call(
             functools.partial(fused_kernel, layers, rows_n, cols_n),
             out_shape=(
-                jax.ShapeDtypeStruct((1, piece, right), F32),
-                jax.ShapeDtypeStruct((SUB_NODES, piece, right), F32),
+                pltpu.VMEM((1, piece, right), F32),
+                pltpu.VMEM((SUB_NODES, piece, right), F32),
             ),
             in_specs=[hbm] * 6 + [smem] * 2,
             out_specs=(vmem, vmem),
             scratch_shapes=[
-                pltpu.VMEM(anc_lower.shape, BF),
-                pltpu.VMEM(anc_upper.shape, BF),
+                pltpu.VMEM((rows_n, cut, cut), BF),
+                pltpu.VMEM((cols_n, cut, cut // layers), BF),
                 pltpu.VMEM(sub_lower.shape, BF),
                 pltpu.VMEM(sub_upper.shape, BF),
                 pltpu.VMEM(anc_rhs.shape, BF),
@@ -532,13 +480,14 @@
                 pltpu.VMEM((7, H, peers_n, 1) + vec, BF),
                 pltpu.VMEM((H, 1) + vec, BF),
                 pltpu.VMEM((H, layers * rows_n - 1, 1) + vec, BF),
-                pltpu.VMEM((H, 1) + vec, BF),
+                pltpu.VMEM((1, cut, cut // layers), BF),
+                pltpu.VMEM((layers, cut, cut // layers), BF),
                 pltpu.VMEM((2, cut, right), F32),
                 pltpu.VMEM((H, cols_n, right // H, 2 * piece), BF),
                 pltpu.VMEM((H, cols_n - 1, right // H, 2 * piece), BF),
                 pltpu.SemaphoreType.DMA((8,)),
-                pltpu.SemaphoreType.DMA((H, 11, layers * rows_n)),
-                pltpu.SemaphoreType.DMA((H, 11, layers * rows_n)),
+                pltpu.SemaphoreType.DMA((H, 12, layers * rows_n)),
+                pltpu.SemaphoreType.DMA((H, 12, layers * rows_n)),
             ],
             compiler_params=pltpu.CompilerParams(collective_id=0, has_side_effects=True),
         )(*args)

time: 56.8 us -> 52 us (0.915)
  Pallas kernels: 53 us -> 50 us
  local copies, waits for them, and re-layouts: 2.91 us -> 1.26 us
    pallas_call x1, Pallas kernels: 53 us -> 50 us  [local_fused(): pl.pallas_call(functools.partial(fused_kernel, layers, rows_n, cols_n), o...]
    unnamed x2, local copies, waits for them, and re-layouts: 2.91 us -> 1.26 us
where the time goes in v3:
time: 52 us; the launch traced here: 51.9 us
  Pallas kernels  50 us (96%)
  local copies, waits for them, and re-layouts  1.26 us (2%)
  between operations  0.64 us (1%)
    pallas_call x1, Pallas kernels, local_fused(): pl.pallas_call(functools.partial(fused_kernel, layers, rows_n, cols_n), o...  50 us
    unnamed x2, local copies, waits for them, and re-layouts  1.26 us

profile of v3, /device:TPU:0, one launch (start us, length us, event | category | flops | bytes accessed | tf_op | source)
XLA Modules:
  0.0 51.9 jit_solution(1850884834495736868)
XLA Ops:
  0.6 50.0 %shard_map.95 = (f32[1,64,64]{2,1,0:T(8,128)S(1)}, f32[3,64,64]{2,1,0:T(8,128)S(1)}) custom-call(bf16[1,256,256]{2,1,0:T(8,128)(2,1)} %anc_lower.1, bf16[1,256,256]{2,1,0:T(8,128)(2,1)} %anc_upper.1, bf16[8,256,256]{2,1,0:T(8,128)(2,1)} %sub_lower.1, bf16[8,256,256]{2,1,0:T(8,128)(2,1)} %sub_upper.1, bf16[1,64,256]{2,1,0:T(8,128)(2,1)} %bitcast.4, ...), custom_call_target="tpu_custom_call" | custom-call | tf_op jit(solution)/shard_map/pallas_call | solution.py:462
  50.6 0.6 %copy.12 = f32[1,64,64]{2,1,0:T(8,128)} copy(f32[1,64,64]{2,1,0:T(8,128)S(1)} %get-tuple-element.2) | data formatting | bytes 32768
  51.2 0.6 %copy.13 = f32[3,64,64]{2,1,0:T(8,128)} copy(f32[3,64,64]{2,1,0:T(8,128)S(1)} %get-tuple-element.3) | data formatting | bytes 98304

commit v4 on v3

--- a/solution.py
+++ b/solution.py
@@ -245,6 +245,24 @@
     gz = lax.axis_index("gz")
     row = lax.axis_index("row")
     col = lax.axis_index("col")
+    def row_peer(j):
+        return (gz, lax.rem(row + j, rows_n), col)
+
+    def col_peer(j):
+        return (gz, row, lax.rem(col + j, cols_n))
+
+    barrier = pltpu.get_barrier_semaphore()
+    peers = [row_peer(j) for j in range(1, rows_n)] + [col_peer(j) for j in range(1, cols_n)]
+    wide = [
+        (lax.rem(gz + g, layers), lax.rem(row + j, rows_n), col)
+        for g in range(layers)
+        for j in range(rows_n)
+        if g or j
+    ]
+    peers = peers + wide[rows_n - 1 :]
+    for peer in peers:
+        pl.semaphore_signal(barrier, inc=1, device_id=peer, device_id_type=MESH)
+
     loads = {}
 
     def load(name, source, target):
@@ -266,24 +284,6 @@
     )
     load("su", sub_upper, su)
 
-    def row_peer(j):
-        return (gz, lax.rem(row + j, rows_n), col)
-
-    def col_peer(j):
-        return (gz, row, lax.rem(col + j, cols_n))
-
-    barrier = pltpu.get_barrier_semaphore()
-    peers = [row_peer(j) for j in range(1, rows_n)] + [col_peer(j) for j in range(1, cols_n)]
-    wide = [
-        (lax.rem(gz + g, layers), lax.rem(row + j, rows_n), col)
-        for g in range(layers)
-        for j in range(rows_n)
-        if g or j
-    ]
-    peers = peers + wide[rows_n - 1 :]
-    for peer in peers:
-        pl.semaphore_signal(barrier, inc=1, device_id=peer, device_id_type=MESH)
-
     started = []
     half = sr.shape[1] // HALVES
     span = [slice(h * half, (h + 1) * half) for h in range(HALVES)]
@@ -338,20 +338,62 @@
     loads["al"].wait()
     loads["au"].wait()
     blocks = send(0, 4, lambda j: al.at[0], lambda j: al.at[j + 1], row_list)
-    blocks = blocks + send(0, 5, lambda j: au.at[0], lambda j: au.at[j + 1], col_list)
+
+    def hop(right, stage):
+        step_id = 5 if right else 10
+        to = col + 1 if right else col + cols_n - 1
+        copy = pltpu.make_async_remote_copy(
+            src_ref=au.at[stage - 1 if right else (cols_n - stage + 1) % cols_n],
+            dst_ref=au.at[stage if right else cols_n - stage],
+            send_sem=send_sem.at[0, step_id, cols_n + stage - 1],
+            recv_sem=recv_sem.at[0, step_id, cols_n + stage - 1],
+            device_id=(gz, row, lax.rem(to, cols_n)),
+            device_id_type=MESH,
+        )
+        if right:
+            return copy, (col + 1 < cols_n) & (col >= stage - 1), col >= stage
+        return copy, (col >= 1) & (col < cols_n - stage + 1), col < cols_n - stage
+
+    def relay(stage):
+        for right in (True, False):
+            if stage > 1:
+                before, unused, gets = hop(right, stage - 1)
+
+                @pl.when(gets)
+                def arrived():
+                    before.wait_recv()
+
+            if stage < cols_n:
+                copy, sends, unused = hop(right, stage)
+
+                @pl.when(sends)
+                def forward():
+                    copy.start()
+
+    relay(1)
     loads["low"].wait()
     y = [None] * HALVES
     for h in each:
         y[h] = [v.astype(BF) for v in finish(step[h])]
         change = low[2] * times_t(y[h][0], sl[5]) + low[4] * times_t(y[h][1], sl[7])
         step[h] = begin(h, 1, [change], row_list, one_send.at[0], one_recv.at[0])
+    for stage in range(2, cols_n - 1):
+        relay(stage)
     loads["e0"].wait()
     to_anc = [low[1] * times_t(y[h][0], sl[4]) + low[3] * times_t(y[h][1], sl[6]) for h in each]
 
     for h in each:
         r0 = (sr[0, span[h]].astype(F32) - finish(step[h])[0]).astype(BF)
         step[h] = begin(h, 2, [times(r0, sl[0])], col_list, one_send.at[1], one_recv.at[1])
+    relay(cols_n - 1)
     loads["ar"].wait()
+    for h in each:
+        y0 = finish(step[h])[0].astype(BF)
+        y[h] = [y0] + y[h]
+        step[h] = begin(
+            h, 3, [to_anc[h] + low[0] * times_t(y0, sl[3])], wide, all_send, all_recv
+        )
+    relay(cols_n)
     for copy in blocks:
         copy.wait_recv()
     product = jnp.zeros((al.shape[1], width), F32)
@@ -365,12 +407,6 @@
     blocks = send(
         0, 11, lambda j: product_send.at[0], lambda j: product_recv.at[j + 1], layer_list
     )
-    for h in each:
-        y0 = finish(step[h])[0].astype(BF)
-        y[h] = [y0] + y[h]
-        step[h] = begin(
-            h, 3, [to_anc[h] + low[0] * times_t(y0, sl[3])], wide, all_send, all_recv
-        )
 
     for copy in blocks:
         copy.wait_recv()
@@ -440,6 +476,13 @@
     sub_out[2] = total[piece:]
     for copy in started:
         copy.wait_send()
+    for stage in range(1, cols_n):
+        for right in (True, False):
+            copy, sends, unused = hop(right, stage)
+
+            @pl.when(sends)
+            def sent():
+                copy.wait_send()
 
 
 def fused(mesh):

time: 52 us -> 50.9 us (0.979)
  Pallas kernels: 50 us -> 48.9 us
    pallas_call x1, Pallas kernels: 50 us -> 48.9 us  [local_fused(): pl.pallas_call(functools.partial(fused_kernel, layers, rows_n, cols_n), o...]
where the time goes in v4:
time: 50.9 us; the launch traced here: 50.8 us
  Pallas kernels  48.9 us (96%)
  local copies, waits for them, and re-layouts  1.26 us (2%)
  between operations  0.64 us (1%)
    pallas_call x1, Pallas kernels, local_fused(): pl.pallas_call(functools.partial(fused_kernel, layers, rows_n, cols_n), o...  48.9 us
    unnamed x2, local copies, waits for them, and re-layouts  1.26 us

profile of v4, /device:TPU:0, one launch (start us, length us, event | category | flops | bytes accessed | tf_op | source)
XLA Modules:
  0.0 50.8 jit_solution(5434771422805144859)
XLA Ops:
  0.6 48.9 %shard_map.95 = (f32[1,64,64]{2,1,0:T(8,128)S(1)}, f32[3,64,64]{2,1,0:T(8,128)S(1)}) custom-call(bf16[1,256,256]{2,1,0:T(8,128)(2,1)} %anc_lower.1, bf16[1,256,256]{2,1,0:T(8,128)(2,1)} %anc_upper.1, bf16[8,256,256]{2,1,0:T(8,128)(2,1)} %sub_lower.1, bf16[8,256,256]{2,1,0:T(8,128)(2,1)} %sub_upper.1, bf16[1,64,256]{2,1,0:T(8,128)(2,1)} %bitcast.4, ...), custom_call_target="tpu_custom_call" | custom-call | tf_op jit(solution)/shard_map/pallas_call | solution.py:505
  49.5 0.6 %copy.12 = f32[1,64,64]{2,1,0:T(8,128)} copy(f32[1,64,64]{2,1,0:T(8,128)S(1)} %get-tuple-element.2) | data formatting | bytes 32768
  50.1 0.6 %copy.13 = f32[3,64,64]{2,1,0:T(8,128)} copy(f32[3,64,64]{2,1,0:T(8,128)S(1)} %get-tuple-element.3) | data formatting | bytes 98304
